TPU v7x, 32 devices: a whole 2x2x4 slice. The times are simulated.
32 devices in a mesh: heads: 2 (over x), wide: 16 (over z, y, core).
Axes of the slice: x: 2, y: 2, z: 4, core: 2. Of those that a mesh axis runs over, the one named last changes fastest.
Arguments:
- tokens: bfloat16 [32, 1024, 768], P(('heads', 'wide')), may hold values from -36 to 36
- cotangent: bfloat16 [32, 1024, 768], P(('heads', 'wide')), may hold values from -11 to 11
- lengths: int32 [32], P(('heads', 'wide')), may hold values from 196 to 1024, as said below
- step_count: int32 [1], replicated, may hold values from 2 to 20
- attend_weights: float32 [3, 768, 768], P(None, 'wide', 'heads'), may hold values from -0.21875 to 0.21875
- output_weights: float32 [768, 768], P('heads', 'wide'), may hold values from -7 to 7
- expand_weights: float32 [768, 3072], P('wide', 'heads'), may hold values from -0.21875 to 0.21875
- reduce_weights: float32 [3072, 768], P('heads', 'wide'), may hold values from -1 to 1
- expand_bias: float32 [3072], P(('heads', 'wide')), may hold values from -3 to 3
- norm_gains: float32 [3, 768], P(None, ('heads', 'wide')), may hold values from 0.1 to 1.9
- first_attend: float32 [3, 768, 768], P(None, 'wide', 'heads'), may hold values from -1.25 to 1.25
- first_output: float32 [768, 768], P('heads', 'wide'), may hold values from -0.25 to 0.25
- first_expand: float32 [768, 3072], P('wide', 'heads'), may hold values from -0.875 to 0.875
- first_reduce: float32 [3072, 768], P('heads', 'wide'), may hold values from -2 to 2
- first_bias: float32 [3072], P(('heads', 'wide')), may hold values from -0.875 to 0.875
- first_gains: float32 [3, 768], P(None, ('heads', 'wide')), may hold values from -3 to 3
- second_attend: float32 [3, 768, 768], P(None, 'wide', 'heads'), may hold values from 0.1048576 to 1.703936
- second_output: float32 [768, 768], P('heads', 'wide'), may hold values from 0.0032768 to 0.0524288
- second_expand: float32 [768, 3072], P('wide', 'heads'), may hold values from 0.0458752 to 0.753664
- second_reduce: float32 [3072, 768], P('heads', 'wide'), may hold values from 0.2195456 to 3.60448
- second_bias: float32 [3072], P(('heads', 'wide')), may hold values from 0.0458752 to 0.753664
- second_gains: float32 [3, 768], P(None, ('heads', 'wide')), may hold values from 0.524288 to 8.192
- average_attend: float32 [3, 768, 768], P(None, 'wide', 'heads'), may hold values from -0.21875 to 0.21875
- average_output: float32 [768, 768], P('heads', 'wide'), may hold values from -1.75 to 1.75
- average_expand: float32 [768, 3072], P('wide', 'heads'), may hold values from -0.21875 to 0.21875
- average_reduce: float32 [3072, 768], P('heads', 'wide'), may hold values from -0.109375 to 0.109375
- average_bias: float32 [3072], P(('heads', 'wide')), may hold values from -3 to 3
- average_gains: float32 [3, 768], P(None, ('heads', 'wide')), may hold values from 0.1 to 1.9
Outputs:
- block_output: float32 [32, 1024, 768], P(('heads', 'wide'))
- token_gradient: float32 [32, 1024, 768], P(('heads', 'wide'))
- gradient_norm: float32 [1], replicated
- clip_attend: float32 [3, 768, 768], P(None, 'wide', 'heads')
- mean_attend: float32 [3, 768, 768], P(None, 'wide', 'heads')
- square_attend: float32 [3, 768, 768], P(None, 'wide', 'heads')
- weight_attend: float32 [3, 768, 768], P(None, 'wide', 'heads')
- smooth_attend: float32 [3, 768, 768], P(None, 'wide', 'heads')
- clip_output: float32 [768, 768], P('heads', 'wide')
- mean_output: float32 [768, 768], P('heads', 'wide')
- square_output: float32 [768, 768], P('heads', 'wide')
- weight_output: float32 [768, 768], P('heads', 'wide')
- smooth_output: float32 [768, 768], P('heads', 'wide')
- clip_expand: float32 [768, 3072], P('wide', 'heads')
- mean_expand: float32 [768, 3072], P('wide', 'heads')
- square_expand: float32 [768, 3072], P('wide', 'heads')
- weight_expand: float32 [768, 3072], P('wide', 'heads')
- smooth_expand: float32 [768, 3072], P('wide', 'heads')
- clip_reduce: float32 [3072, 768], P('heads', 'wide')
- mean_reduce: float32 [3072, 768], P('heads', 'wide')
- square_reduce: float32 [3072, 768], P('heads', 'wide')
- weight_reduce: float32 [3072, 768], P('heads', 'wide')
- smooth_reduce: float32 [3072, 768], P('heads', 'wide')
- clip_bias: float32 [3072], P(('heads', 'wide'))
- mean_bias: float32 [3072], P(('heads', 'wide'))
- square_bias: float32 [3072], P(('heads', 'wide'))
- weight_bias: float32 [3072], P(('heads', 'wide'))
- smooth_bias: float32 [3072], P(('heads', 'wide'))
- clip_gains: float32 [3, 768], P(None, ('heads', 'wide'))
- mean_gains: float32 [3, 768], P(None, ('heads', 'wide'))
- square_gains: float32 [3, 768], P(None, ('heads', 'wide'))
- weight_gains: float32 [3, 768], P(None, ('heads', 'wide'))
- smooth_gains: float32 [3, 768], P(None, ('heads', 'wide'))
Inputs may be any that keep to these rules, and one draw needn't show every extreme that they name: `lengths`: each image has 1024 * 196 // 1024 (at least 1), 576 or 1024 valid tokens; image 0 has 1024, image 1 the fewest.
All inputs are finite; a program needn't handle non-finite values.
Results may differ from a plain program's by a relative error of at most 0.011.
Values may be sent and summed in bfloat16 or wider, within the bound.
A program may use at most 192 MiB of HBM per device.

v0:
```python
from functools import partial
import math

import jax
import jax.numpy as jnp
from jax import lax
from jax.experimental import pallas as pl
from jax.experimental.pallas import tpu as pltpu
from jax.sharding import PartitionSpec as P

D = 768
HEADS = 12
HEAD_DIM = 64
FF = 3072
HALF_E = D // 2
HALF_F = FF // 2
PAIR = 128
PAIRS = HALF_E // PAIR
CHUNK = 512
CHUNKS = HALF_F // CHUNK
QUERY_ROWS = 512
ROWS = 256
BF = jnp.bfloat16
F32 = jnp.float32

NORM_EPS = 1e-06
MASKED = -1e30
BETA_FIRST = 0.9
BETA_SECOND = 0.95
AVERAGE_CAP = 0.9999
ADAM_EPS = 1e-08
RATES = (0.03, 0.2, 0.03, 0.015, 0.3, 0.3)
DECAYS = (0.05, 0.05, 0.05, 0.05, 0.0, 0.0)


def dot(left, right, left_dim, right_dim):
    return lax.dot_general(
        left, right, (((left_dim,), (right_dim,)), ((), ())), preferred_element_type=F32
    )


def row_norm(values):
    center = values - jnp.mean(values, axis=-1, keepdims=True)
    inverse = lax.rsqrt(jnp.mean(center * center, axis=-1, keepdims=True) + NORM_EPS)
    return center * inverse, inverse


def head_mean(values):
    width = values.shape[1]
    row = lax.broadcasted_iota(jnp.int32, (width, width), 0) // HEAD_DIM
    column = lax.broadcasted_iota(jnp.int32, (width, width), 1) // HEAD_DIM
    block = jnp.where(row == column, 1.0 / HEAD_DIM, 0.0).astype(BF)
    high = values.astype(BF)
    rest = (values - high.astype(F32)).astype(BF)
    return dot(high, block, 1, 0) + dot(rest, block, 1, 0)


def head_norm(values):
    center = values - head_mean(values)
    inverse = lax.rsqrt(head_mean(center * center) + NORM_EPS)
    return center * inverse, inverse


def head_norm_back(upstream, normal, inverse):
    return inverse * (upstream - head_mean(upstream) - normal * head_mean(upstream * normal))


def pair_attention(query, keyed, value, back_mixed, key_bias):
    rows = query.shape[0]
    lane = lax.broadcasted_iota(jnp.int32, (rows, PAIR), 1)
    low = lane < HEAD_DIM
    first = lane == 0
    zero = jnp.zeros((rows, PAIR), BF)
    one_lane = jnp.where(first, 1.0, 0.0).astype(BF)
    bias_lane = jnp.where(first, key_bias, 0.0).astype(BF)
    query_wide = jnp.concatenate([query, one_lane], axis=1)
    value_wide = jnp.concatenate([value, jnp.ones((rows, PAIR), BF)], axis=1)
    blocks = rows // QUERY_ROWS
    mixed = [[None] * blocks for _ in range(2)]
    back_query = [[None] * blocks for _ in range(2)]
    back_keyed = None
    back_value = None
    lane_q = lane[:QUERY_ROWS]
    low_q = low[:QUERY_ROWS]
    for head in range(2):
        mine = low if head == 0 else ~low
        mine_q = mine[:QUERY_ROWS]
        key_wide = jnp.concatenate([jnp.where(mine, keyed, zero), bias_lane], axis=1)
        query_mine = jnp.where(mine, query, zero)
        for block in range(blocks):
            cut = slice(block * QUERY_ROWS, (block + 1) * QUERY_ROWS)
            expo = jnp.exp(dot(query_wide[cut], key_wide, 1, 1))
            expo_low = expo.astype(BF)
            sums = dot(expo_low, value_wide, 1, 0)
            inverse = 1.0 / sums[:, PAIR:]
            rows_mixed = sums[:, :PAIR] * inverse
            scaled = jnp.where(mine_q, back_mixed[cut].astype(F32) * inverse, 0.0).astype(BF)
            inner = jnp.sum(rows_mixed * scaled.astype(F32), axis=1, keepdims=True)
            inner_high = inner.astype(BF).astype(F32)
            inner_lanes = jnp.where(
                lane_q == 0, -inner_high, jnp.where(lane_q == 1, inner_high - inner, 0.0)
            ).astype(BF)
            centered = dot(jnp.concatenate([scaled, inner_lanes], axis=1), value_wide, 1, 1)
            back_scores = (expo * centered).astype(BF)
            mixed[head][block] = rows_mixed
            back_query[head][block] = dot(back_scores, keyed, 1, 0)
            add_keyed = dot(query_mine[cut], back_scores, 0, 0)
            add_value = dot(scaled, expo_low, 0, 0)
            back_keyed = add_keyed if back_keyed is None else back_keyed + add_keyed
            back_value = add_value if back_value is None else back_value + add_value
    join = lambda parts: jnp.concatenate(
        [jnp.where(low_q, parts[0][block], parts[1][block]) for block in range(blocks)], axis=0
    )
    return join(mixed).astype(BF), join(back_query), back_keyed, back_value


def attention_scratch(slots):
    rows = [pltpu.VMEM((2, slots, PAIR), BF)] * 4 + [pltpu.VMEM((2, slots, PAIR), F32)] * 5
    return rows + [pltpu.VMEM((2, PAIR, slots), F32)]


def attention_section(
    weights, normed, upstream, query_gain, key_gain, key_bias, out_ref, back_ref, work, store,
    pause=lambda place: None,
):
    (
        query_ref, key_ref, value_ref, back_mixed_ref,
        query_hat_ref, query_inv_ref, key_hat_ref, key_inv_ref, back_query_ref, back_keyed_ref,
    ) = work
    three = 3 * PAIR
    halves = (slice(0, PAIR), slice(PAIR, 2 * PAIR))
    both = [weights(half) for half in range(2)]
    into = jnp.concatenate([part[:, :three] for part in both], axis=1)
    out = jnp.concatenate([part[:, three:] for part in both], axis=1)
    projected = dot(normed, into, 1, 0)
    back_mixed = dot(upstream, out, 1, 0).astype(BF)
    pick = lambda place: jnp.concatenate(
        [
            projected[:, place * PAIR : (place + 1) * PAIR],
            projected[:, three + place * PAIR : three + (place + 1) * PAIR],
        ],
        axis=1,
    )
    query_hat, query_inv = head_norm(pick(0))
    key_hat, key_inv = head_norm(pick(1))
    query = (query_hat * query_gain).astype(BF)
    query = (query.astype(F32) * HEAD_DIM ** (-0.5)).astype(BF)
    keyed = (key_hat * key_gain).astype(BF)
    value = pick(2).astype(BF)
    for half, cut in enumerate(halves):
        for ref, rows in (
            (query_ref, query), (key_ref, keyed), (value_ref, value), (back_mixed_ref, back_mixed),
            (query_hat_ref, query_hat), (query_inv_ref, query_inv),
            (key_hat_ref, key_hat), (key_inv_ref, key_inv),
        ):
            ref[half] = rows[:, cut]

    def one_pair(half, carry):
        for place in range(2):
            pl.when(half == place)(partial(pause, place))
        mixed, back_query_ref[half], back_keyed_ref[half], back_value = pair_attention(
            query_ref[half], key_ref[half], value_ref[half], back_mixed_ref[half], key_bias
        )
        query_ref[half] = mixed
        value_ref[half] = back_value.T.astype(BF)
        return carry

    lax.fori_loop(0, 2, one_pair, 0)
    pause(2)
    whole = lambda ref: jnp.concatenate([ref[0], ref[1]], axis=1)
    both = [weights(half) for half in range(2)]
    into = jnp.concatenate([part[:, :three] for part in both], axis=1)
    out = jnp.concatenate([part[:, three:] for part in both], axis=1)
    mixed = whole(query_ref)
    query_hat, key_hat = whole(query_hat_ref), whole(key_hat_ref)
    back_qn = whole(back_query_ref) * HEAD_DIM ** (-0.5)
    back_kn = jnp.concatenate([back_keyed_ref[0].T, back_keyed_ref[1].T], axis=1)
    query_gain_back = jnp.sum(back_qn * query_hat, axis=0, keepdims=True)
    key_gain_back = jnp.sum(back_kn * key_hat, axis=0, keepdims=True)
    back_query = head_norm_back(back_qn * query_gain, query_hat, whole(query_inv_ref)).astype(BF)
    back_keyed = head_norm_back(back_kn * key_gain, key_hat, whole(key_inv_ref)).astype(BF)
    back_into = jnp.concatenate(
        [
            part
            for half, cut in enumerate(halves)
            for part in (back_query[:, cut], back_keyed[:, cut], value_ref[half])
        ],
        axis=1,
    )
    grad_into = dot(normed, back_into, 0, 0).astype(BF)
    grad_out = dot(upstream, mixed, 0, 0).astype(BF)
    grads = [
        jnp.concatenate([grad_into[:, half * three : (half + 1) * three], grad_out[:, cut]], axis=1)
        for half, cut in enumerate(halves)
    ]
    store(grads, query_gain_back, key_gain_back)
    pause(3)
    out_ref[...] += dot(mixed, out, 1, 1)
    back_ref[...] += dot(back_into, into, 1, 1)


def mlp_section(weights, normed, upstream, bias, out_ref, back_ref):
    expand = weights[:, :CHUNK]
    reduce = weights[:, CHUNK:]
    pre = dot(normed, expand, 1, 0) + bias
    back_hidden = dot(upstream, reduce, 1, 0)
    phi = 0.5 * (1.0 + lax.erf(pre * math.sqrt(0.5)))
    density = jnp.exp(-0.5 * pre * pre) * (1.0 / math.sqrt(2.0 * math.pi))
    hidden = (pre * phi).astype(BF)
    back_pre = (back_hidden * (phi + pre * density)).astype(BF)
    out_ref[...] += dot(hidden, reduce, 1, 1)
    back_ref[...] += dot(back_pre, expand, 1, 1)
    grads = [dot(normed, back_pre, 0, 0).astype(BF), dot(upstream, hidden, 0, 0).astype(BF)]
    return jnp.concatenate(grads, axis=1), jnp.sum(back_pre.astype(F32), axis=0, keepdims=True)


def over_rows(slots, act):
    def one(block, carry):
        act(pl.ds(pl.multiple_of(block * ROWS, ROWS), ROWS))
        return carry

    lax.fori_loop(0, slots // ROWS, one, 0)


def below(length_ref, rows):
    place = lax.broadcasted_iota(jnp.int32, (rows.size, 1), 0) + rows.start
    return place < length_ref[0]


def start_input(
    length_ref, tokens_ref, cotangent_ref, gains_ref, normed_ref, upstream_ref, out_ref, back_ref
):
    def one(rows):
        inputs = tokens_ref[rows, :].astype(F32)
        input_hat, _ = row_norm(inputs)
        normed_ref[rows, :] = (input_hat * gains_ref[0:1, :]).astype(BF)
        upstream_ref[rows, :] = jnp.where(
            below(length_ref, rows), cotangent_ref[rows, :].astype(F32), 0.0
        ).astype(BF)
        out_ref[rows, :] = inputs
        back_ref[rows, :] = jnp.zeros_like(inputs)

    over_rows(tokens_ref.shape[0], one)


def finish_input(tokens_ref, gains_ref, upstream_ref, back_ref, gains_back_ref):
    gains_back_ref[0:1, :] = jnp.zeros_like(gains_back_ref[0:1, :])

    def one(rows):
        input_hat, input_inv = row_norm(tokens_ref[rows, :].astype(F32))
        back_normed = back_ref[rows, :]
        gains_back_ref[0:1, :] += jnp.sum(back_normed * input_hat, axis=0, keepdims=True)
        scaled = back_normed * gains_ref[0:1, :]
        back_ref[rows, :] = upstream_ref[rows, :].astype(F32) + input_inv * (
            scaled
            - jnp.mean(scaled, axis=-1, keepdims=True)
            - input_hat * jnp.mean(scaled * input_hat, axis=-1, keepdims=True)
        )

    over_rows(tokens_ref.shape[0], one)


def local_kernel(
    length_ref, tokens_ref, cotangent_ref, gains_ref, bias_ref, pair_ref, chunk_ref,
    out_ref, back_ref, grad_pair_ref, grad_chunk_ref, bias_back_ref, gains_back_ref,
    normed_ref, upstream_ref, *work,
):
    index = pl.program_id(0)

    @pl.when(index == 0)
    def _():
        start_input(
            length_ref, tokens_ref, cotangent_ref, gains_ref, normed_ref, upstream_ref, out_ref, back_ref
        )

    is_pair = (index == 0) | (index > 2 * CHUNKS)

    @pl.when(is_pair)
    def _():
        unit = jnp.where(index == 0, 0, index - 2 * CHUNKS)
        starts = [pl.multiple_of(half * HALF_E + unit * PAIR, PAIR) for half in range(2)]
        gain_of = lambda row: jnp.concatenate(
            [gains_ref[row : row + 1, pl.ds(start, PAIR)] for start in starts], axis=1
        )
        place = lax.broadcasted_iota(jnp.int32, (tokens_ref.shape[0], 1), 0)

        def store(grads, query_back, key_back):
            for half in range(2):
                grad_pair_ref[0, half] = grads[half]
                cut = slice(half * PAIR, (half + 1) * PAIR)
                gains_back_ref[1:2, pl.ds(starts[half], PAIR)] = query_back[:, cut]
                gains_back_ref[2:3, pl.ds(starts[half], PAIR)] = key_back[:, cut]

        attention_section(
            lambda half: pair_ref[0, half], normed_ref[...], upstream_ref[...],
            gain_of(1), gain_of(2), jnp.where(place < length_ref[0], 0.0, MASKED), out_ref, back_ref, work,
            store,
        )

    @pl.when(~is_pair)
    def _():
        unit = (index - 1) // 2
        half = lax.rem(index - 1, 2)
        start = pl.multiple_of(half * HALF_F + unit * CHUNK, CHUNK)
        grad, bias_back = mlp_section(
            chunk_ref[0, 0], normed_ref[...], upstream_ref[...],
            bias_ref[0:1, pl.ds(start, CHUNK)], out_ref, back_ref,
        )
        grad_chunk_ref[0, 0] = grad
        bias_back_ref[0:1, pl.ds(start, CHUNK)] = bias_back

    @pl.when(index == PAIRS + 2 * CHUNKS - 1)
    def _():
        finish_input(tokens_ref, gains_ref, upstream_ref, back_ref, gains_back_ref)


def local_block(length, tokens, cotangent, gains, bias, pair_weights, chunk_weights):
    slots = tokens.shape[0]
    steps = PAIRS + 2 * CHUNKS
    whole = lambda shape: pl.BlockSpec(shape, lambda index: (0,) * len(shape))
    pair_at = lambda index: (jnp.maximum(index - 2 * CHUNKS, 0), 0, 0, 0)

    def chunk_at(index):
        flat = jnp.clip(index - 1, 0, 2 * CHUNKS - 1)
        return (flat // 2, lax.rem(flat, 2), 0, 0)

    pair_spec = pl.BlockSpec((1, 2, D, 4 * PAIR), pair_at)
    chunk_spec = pl.BlockSpec((1, 1, D, 2 * CHUNK), chunk_at)
    return pl.pallas_call(
        local_kernel,
        grid=(steps,),
        in_specs=[
            pl.BlockSpec(memory_space=pltpu.SMEM),
            whole((slots, D)), whole((slots, D)), whole((3, D)), whole((1, FF)), pair_spec, chunk_spec,
        ],
        out_specs=[
            whole((slots, D)), whole((slots, D)), pair_spec, chunk_spec, whole((1, FF)), whole((3, D)),
        ],
        out_shape=[
            jax.ShapeDtypeStruct((slots, D), F32),
            jax.ShapeDtypeStruct((slots, D), F32),
            jax.ShapeDtypeStruct((PAIRS, 2, D, 4 * PAIR), BF),
            jax.ShapeDtypeStruct((CHUNKS, 2, D, 2 * CHUNK), BF),
            jax.ShapeDtypeStruct((1, FF), F32),
            jax.ShapeDtypeStruct((3, D), F32),
        ],
        scratch_shapes=[pltpu.VMEM((slots, D), BF), pltpu.VMEM((slots, D), BF)]
        + attention_scratch(slots),
        compiler_params=pltpu.CompilerParams(vmem_limit_bytes=60 << 20),
        name="local_block",
    )(length, tokens, cotangent, gains, bias, pair_weights, chunk_weights)


PAIR_UNITS = (0, 1, 5)
CHUNK_UNITS = (2, 3, 4)
UNITS = 6
SECTIONS = PAIRS + 2 * CHUNKS
FIRST_CHUNK = 2
LAST_PAIR = SECTIONS - 1
GATHER_COPIES = 11
SCATTER_COPIES = 8
MESH = pl.DeviceIdType.MESH


class Traffic:
    def __init__(self, refs):
        self.__dict__.update(refs)
        self.deep = self.pair.shape[2]
        self.h = lax.axis_index("heads")
        wide = lax.axis_index("wide")
        self.c = lax.rem(wide, 2)
        self.b = lax.rem(wide // 2, 2)
        self.a = wide // 4

    def buffer(self, unit):
        if unit in PAIR_UNITS:
            return self.pair.at[PAIR_UNITS.index(unit)]
        return self.chunk.at[CHUNK_UNITS.index(unit)]

    def own(self, unit):
        if unit in PAIR_UNITS:
            return self.pair_own.at[PAIR_UNITS.index(unit)]
        return self.chunk_own.at[CHUNK_UNITS.index(unit)]

    def landing(self, unit, stage):
        pair = unit in PAIR_UNITS
        landing = (self.pair_landing if pair else self.chunk_landing)[stage]
        return landing.at[(PAIR_UNITS if pair else CHUNK_UNITS).index(unit) % landing.shape[0]]

    def device(self, h=None, a=None, b=None, c=None):
        h = self.h if h is None else h
        a = self.a if a is None else a
        b = self.b if b is None else b
        c = self.c if c is None else c
        return (h, (a * 2 + b) * 2 + c)

    def beside(self, axis):
        if axis == "h":
            return self.device(h=1 - self.h)
        if axis == "b":
            return self.device(b=1 - self.b)
        return self.device(c=1 - self.c)

    def along(self, step):
        return self.device(a=lax.rem(self.a + step, self.deep))

    def copy(self, source, target, sems, unit, slot, device):
        send, recv = sems
        return pltpu.make_async_remote_copy(
            src_ref=source, dst_ref=target, send_sem=send.at[unit, slot], recv_sem=recv.at[unit, slot],
            device_id=device, device_id_type=MESH,
        )

    def gather_copy(self, unit, slot):
        buf, own, half = self.buffer(unit), self.own(unit), self.deep // 2
        h, a, b, c = self.h, self.a, self.b, self.c
        if slot < self.deep - 1:
            return self.copy(own, buf.at[h, a, b, c], self.gather_sems, unit, slot, self.along(slot + 1))
        slot -= self.deep - 1
        region, device = (
            (lambda r: r.at[h, :, b, c], self.beside("h")),
            (lambda r: r.at[h, :, b, c], self.beside("b")),
            (lambda r: r.at[1 - h, pl.ds(0, half), b, c], self.beside("b")),
            (lambda r: r.at[h, pl.ds(half, self.deep - half), 1 - b, c], self.beside("h")),
            (lambda r: r.at[h, :, b, c], self.beside("c")),
            (lambda r: r.at[1 - h, :, b, c], self.beside("c")),
            (lambda r: r.at[h, :, 1 - b, c], self.beside("c")),
            (lambda r: r.at[1 - h, :, 1 - b, c], self.beside("c")),
        )[slot]
        return self.copy(
            region(buf), region(buf), self.gather_sems, unit, slot + self.deep - 1, device
        )

    def gather_start(self, unit, slots):
        for slot in slots:
            self.gather_copy(unit, slot).start()

    def gather_wait(self, unit, slots):
        for slot in slots:
            self.gather_copy(unit, slot).wait_recv()

    def local_copy(self, unit):
        return pltpu.make_async_copy(
            self.own(unit), self.buffer(unit).at[self.h, self.a, self.b, self.c], self.local_sem.at[unit]
        )

    def gather_deep(self, unit):
        self.gather_start(unit, range(self.deep - 1))
        self.local_copy(unit).start()

    def gather_sides(self, unit):
        n = self.deep - 1
        self.local_copy(unit).wait()
        self.gather_wait(unit, range(n))
        self.gather_start(unit, (n, n + 1, n + 4))

    def gather_forward(self, unit):
        n = self.deep - 1
        self.gather_wait(unit, (n, n + 1))
        self.gather_start(unit, (n + 2, n + 3, n + 5, n + 6))

    def gather_core(self, unit):
        n = self.deep - 1
        self.gather_wait(unit, (n + 2, n + 3))
        self.gather_start(unit, (n + 7,))

    def gather_done(self, unit):
        n = self.deep - 1
        self.gather_wait(unit, range(n + 4, n + 8))
        for slot in range(n + 8):
            self.gather_copy(unit, slot).wait_send()

    def scatter_copy(self, unit, slot):
        buf, half = self.buffer(unit), self.deep // 2
        h, a, b, c = self.h, self.a, self.b, self.c
        land = lambda stage: self.landing(unit, stage)
        rest = self.deep - half
        if slot >= 5:
            step = slot - 4
            source = buf.at[h, lax.rem(a + step, self.deep), b, c]
            target, device = land(3).at[step - 1], self.along(step)
        else:
            source, target, device = (
                lambda: (buf.at[:, :, :, 1 - c], land(0), self.beside("c")),
                lambda: (buf.at[1 - h, pl.ds(0, half), 1 - b, c], land(1).at[pl.ds(0, half)], self.beside("b")),
                lambda: (buf.at[1 - h, pl.ds(half, rest), 1 - b, c], land(1).at[pl.ds(half, rest)], self.beside("h")),
                lambda: (buf.at[1 - h, :, b, c], land(2).at[0], self.beside("h")),
                lambda: (buf.at[h, :, 1 - b, c], land(2).at[1], self.beside("b")),
            )[slot]()
        return self.copy(source, target, self.scatter_sems, unit, slot, device)

    def scatter_start(self, unit, slots):
        for slot in slots:
            self.scatter_copy(unit, slot).start()

    def scatter_wait(self, unit, slots):
        for slot in slots:
            self.scatter_copy(unit, slot).wait_recv()

    def add(self, unit, where, *parts):
        buf = self.buffer(unit)
        total = buf[where].astype(F32)
        for part in parts:
            total = total + part.astype(F32)
        buf[where] = total.astype(BF)

    def scatter_core(self, unit):
        self.scatter_start(unit, (0,))

    def scatter_far(self, unit):
        h, b, c = self.h, self.b, self.c
        self.scatter_wait(unit, (0,))
        got = self.landing(unit, 0)
        far = (1 - h, slice(None), 1 - b)
        self.add(unit, far + (c,), got[far])
        self.scatter_start(unit, (1, 2))
        for near in ((1 - h, slice(None), b), (h, slice(None), 1 - b), (h, slice(None), b)):
            self.add(unit, near + (c,), got[near])

    def scatter_sides(self, unit):
        h, b, c, half = self.h, self.b, self.c, self.deep // 2
        self.scatter_wait(unit, (1, 2))
        got = self.landing(unit, 1)
        self.add(unit, (1 - h, slice(0, half), b, c), got[0:half])
        self.add(unit, (h, slice(half, self.deep), 1 - b, c), got[half : self.deep])
        self.scatter_start(unit, (3, 4))

    def scatter_deep(self, unit):
        self.scatter_wait(unit, (3, 4))
        got = self.landing(unit, 2)
        self.add(unit, (self.h, slice(None), self.b, self.c), got[0], got[1])
        self.scatter_start(unit, range(5, 4 + self.deep))

    def scatter_done(self, unit):
        self.scatter_wait(unit, range(5, 4 + self.deep))
        got = self.landing(unit, 3)
        total = self.buffer(unit)[self.h, self.a, self.b, self.c].astype(F32)
        for step in range(self.deep - 1):
            total = total + got[step].astype(F32)
        if unit in PAIR_UNITS:
            self.pair_sum[PAIR_UNITS.index(unit)] = total
        else:
            self.chunk_sum[CHUNK_UNITS.index(unit)] = total
        self.squares[...] += jnp.full(self.squares.shape, jnp.sum(total * total), F32)
        for slot in range(4 + self.deep):
            self.scatter_copy(unit, slot).wait_send()

    def everyone(self, act):
        wides = lax.axis_size("wide")
        count = wides * lax.axis_size("heads")
        me = self.h * wides + lax.axis_index("wide")

        def one(step, carry):
            flat = lax.rem(me + step, count)
            act(flat, (flat // wides, lax.rem(flat, wides)))
            return carry

        lax.fori_loop(1, count, one, 0)

    def small_copy(self, place, source, target, device):
        send, recv = self.small_sems
        return pltpu.make_async_remote_copy(
            src_ref=source, dst_ref=target, send_sem=send.at[place], recv_sem=recv.at[place],
            device_id=device, device_id_type=MESH,
        )

    def small_send(self, place, source_of, target):
        me = self.h * lax.axis_size("wide") + lax.axis_index("wide")
        self.everyone(
            lambda flat, device: self.small_copy(place, source_of(flat), target.at[me], device).start()
        )
        pltpu.make_async_copy(source_of(me), target.at[me], self.small_local.at[place]).start()

    def small_wait(self, place, source_of, target):
        me = self.h * lax.axis_size("wide") + lax.axis_index("wide")
        others = pl.ds(0, target.shape[0] - 1)
        whole = self.small_copy(place, target.at[others], target.at[others], self.beside("c"))
        whole.wait_recv()
        whole.wait_send()
        pltpu.make_async_copy(source_of(me), target.at[me], self.small_local.at[place]).wait()


def spread_matrix(lanes, width, period):
    lane = lax.broadcasted_iota(jnp.int32, (lanes, width), 0).astype(F32)
    column = lax.broadcasted_iota(jnp.int32, (lanes, width), 1).astype(F32)
    place = column - period * jnp.floor((column + 0.5) * (1.0 / period))
    return jnp.where(place == lane, 1.0, 0.0).astype(BF)


def owner_mask(count, width, period):
    owner = lax.broadcasted_iota(jnp.int32, (count, width), 0) * period
    column = lax.broadcasted_iota(jnp.int32, (count, width), 1)
    return (column >= owner) & (column < owner + period)


def split_dot(values, exact, right_dim):
    high = values.astype(BF)
    rest = values - high.astype(F32)
    middle = rest.astype(BF)
    last = (rest - middle.astype(F32)).astype(BF)
    return dot(high, exact, 1, right_dim) + dot(middle, exact, 1, right_dim) + dot(last, exact, 1, right_dim)


def step_kernel(
    length_ref, tokens_ref, cotangent_ref, small_ref, pair_own_ref, chunk_own_ref,
    block_ref, gradient_ref, pair_sum_ref, chunk_sum_ref, extra_ref, total_ref,
    pair_ref, chunk_ref, pair_land0, pair_land1, pair_land2, pair_land3,
    chunk_land0, chunk_land1, chunk_land2, chunk_land3,
    normed_ref, upstream_ref, out_ref, back_ref, gains_ref, bias_ref, gains_back_ref, bias_back_ref,
    smalls_ref, extra_send_ref, extras_ref, norm_ref, squares_ref,
    gather_send, gather_recv, scatter_send, scatter_recv, local_sem, small_send, small_recv, small_local,
    load_sem, *work,
):
    t = Traffic(
        dict(
            pair=pair_ref, chunk=chunk_ref, pair_own=pair_own_ref, chunk_own=chunk_own_ref,
            pair_landing=(pair_land0, pair_land1, pair_land2, pair_land3),
            chunk_landing=(chunk_land0, chunk_land1, chunk_land2, chunk_land3),
            pair_sum=pair_sum_ref, chunk_sum=chunk_sum_ref, squares=squares_ref,
            gather_sems=(gather_send, gather_recv), scatter_sems=(scatter_send, scatter_recv),
            local_sem=local_sem, small_sems=(small_send, small_recv), small_local=small_local,
        )
    )
    slots = normed_ref.shape[0]
    devices = smalls_ref.shape[0]
    gain_width, bias_width = D // devices, FF // devices
    load_tokens = lambda: pltpu.make_async_copy(tokens_ref, normed_ref, load_sem.at[0])
    load_cotangent = lambda: pltpu.make_async_copy(cotangent_ref, upstream_ref, load_sem.at[1])
    load_tokens().start()
    load_cotangent().start()
    barrier = pltpu.get_barrier_semaphore()
    t.everyone(
        lambda flat, device: pl.semaphore_signal(barrier, inc=1, device_id=device, device_id_type=MESH)
    )
    pl.semaphore_wait(barrier, devices - 1)

    t.gather_deep(0)
    small_of = lambda flat: small_ref
    t.small_send(0, small_of, smalls_ref)
    squares_ref[...] = jnp.zeros_like(squares_ref)
    extra_send_ref[...] = jnp.zeros_like(extra_send_ref)
    load_cotangent().wait()
    load_tokens().wait()

    def prepare(rows):
        upstream_ref[rows, :] = jnp.where(
            below(length_ref, rows), upstream_ref[rows, :].astype(F32), 0.0
        ).astype(BF)
        inputs = normed_ref[rows, :].astype(F32)
        out_ref[rows, :] = inputs
        back_ref[rows, :], _ = row_norm(inputs)

    over_rows(slots, prepare)
    t.gather_sides(0)
    t.gather_deep(1)
    t.small_wait(0, small_of, smalls_ref)
    gain_spread = spread_matrix(128, D, gain_width)
    gain_owner = owner_mask(devices, D, gain_width)
    for row in range(3):
        spread = split_dot(smalls_ref[:, row, :], gain_spread, 0)
        gains_ref[row : row + 1, :] = jnp.sum(jnp.where(gain_owner, spread, 0.0), axis=0, keepdims=True)
    bias_spread = spread_matrix(128, FF, bias_width)
    bias_owner = owner_mask(devices, FF, bias_width)
    spread = dot(smalls_ref[:, 3, :].astype(BF), bias_spread, 1, 0)
    bias_ref[...] = jnp.sum(jnp.where(bias_owner, spread, 0.0), axis=0, keepdims=True)
    t.gather_forward(0)

    def scale(rows):
        normed_ref[rows, :] = (back_ref[rows, :] * gains_ref[0:1, :]).astype(BF)
        back_ref[rows, :] = jnp.zeros_like(back_ref[rows, :])

    over_rows(slots, scale)
    t.gather_core(0)
    t.gather_sides(1)
    t.gather_deep(2)
    t.gather_done(0)

    events = {
        (0, -1): [(t.gather_deep, 3)],
        (0, 1): [(t.gather_forward, 1), (t.gather_sides, 2), (t.gather_deep, 4), (t.gather_deep, 5)],
        (0, 2): [(t.gather_core, 1)],
        (0, 3): [(t.gather_done, 1), (t.gather_sides, 3)],
        (1, 0): [(t.gather_forward, 2)],
        (1, 1): [(t.gather_forward, 3), (t.gather_sides, 4)],
        (1, 2): [(t.gather_core, 2)],
        (1, 3): [(t.gather_done, 2), (t.scatter_core, 1), (t.gather_core, 3)],
        (2, -1): [(t.gather_sides, 5), (t.scatter_core, 0)],
        (3, -1): [(t.scatter_far, 1), (t.gather_forward, 4), (t.scatter_far, 0)],
        (4, -1): [(t.gather_done, 3), (t.scatter_core, 2), (t.scatter_sides, 1)],
        (5, -1): [(t.gather_core, 4), (t.scatter_far, 2), (t.gather_forward, 5), (t.scatter_sides, 0)],
        (6, -1): [(t.scatter_core, 3), (t.gather_done, 4)],
        (7, -1): [(t.gather_core, 5), (t.scatter_far, 3), (t.scatter_sides, 2), (t.gather_done, 5)],
        (8, -1): [(t.scatter_core, 4), (t.scatter_deep, 1), (t.scatter_deep, 0)],
        (8, 0): [(t.scatter_far, 4), (t.scatter_sides, 3)],
        (8, 1): [(t.scatter_deep, 2), (t.scatter_sides, 4)],
        (8, 2): [(t.scatter_deep, 3)],
        (8, 3): [(t.scatter_core, 5)],
        ("end", 0): [(t.scatter_far, 5)],
        ("end", 1): [(t.scatter_deep, 4), (t.scatter_sides, 5)],
        ("end", 2): [(t.scatter_done, 1)],
        ("end", 3): [
            (t.scatter_deep, 5), (t.scatter_done, 3), (t.scatter_done, 2), (t.scatter_done, 0),
            (t.scatter_done, 4),
        ],
    }

    def finish(place):
        for act, unit in events["end", place]:
            act(unit)

    def run(index, place, sections):
        for section in sections:
            if (section, place) in events:

                @pl.when(index == section)
                def _():
                    for act, unit in events[section, place]:
                        act(unit)

    def step(index, carry):
        is_pair = (index < FIRST_CHUNK) | (index == LAST_PAIR)
        pair_sections = tuple(range(FIRST_CHUNK)) + (LAST_PAIR,)
        chunk_sections = range(FIRST_CHUNK, LAST_PAIR)

        @pl.when(is_pair)
        def _():
            run(index, -1, pair_sections)
            unit = jnp.where(index == LAST_PAIR, PAIRS - 1, index)
            starts = [pl.multiple_of(half * HALF_E + unit * PAIR, PAIR) for half in range(2)]
            gain_of = lambda row: jnp.concatenate(
                [gains_ref[row : row + 1, pl.ds(start, PAIR)] for start in starts], axis=1
            )

            def store(grads, query_back, key_back):
                for half in range(2):
                    pair_ref[unit, half] = grads[half].reshape(pair_ref.shape[2:])
                    cut = slice(half * PAIR, (half + 1) * PAIR)
                    gains_back_ref[1:2, pl.ds(starts[half], PAIR)] = query_back[:, cut]
                    gains_back_ref[2:3, pl.ds(starts[half], PAIR)] = key_back[:, cut]

            attention_section(
                lambda half: pair_ref[unit, half].reshape(D, 4 * PAIR), normed_ref[...], upstream_ref[...],
                gain_of(1), gain_of(2), jnp.where(below(length_ref, pl.ds(0, slots)), 0.0, MASKED),
                out_ref, back_ref, work, store, lambda place: run(index, place, pair_sections),
            )

        @pl.when(~is_pair)
        def _():
            run(index, -1, chunk_sections)
            unit = (index - FIRST_CHUNK) // 2
            half = lax.rem(index - FIRST_CHUNK, 2)
            start = pl.multiple_of(half * HALF_F + unit * CHUNK, CHUNK)
            grad, bias_back = mlp_section(
                chunk_ref[unit, half].reshape(D, 2 * CHUNK), normed_ref[...], upstream_ref[...],
                bias_ref[0:1, pl.ds(start, CHUNK)], out_ref, back_ref,
            )
            chunk_ref[unit, half] = grad.reshape(chunk_ref.shape[2:])
            bias_back_ref[0:1, pl.ds(start, CHUNK)] = bias_back

        return carry

    lax.fori_loop(0, SECTIONS, step, 0)
    load_tokens().start()
    store_block = pltpu.make_async_copy(out_ref, block_ref, load_sem.at[2])
    store_block.start()
    finish(0)
    load_tokens().wait()
    finish_input(normed_ref, gains_ref, upstream_ref, back_ref, gains_back_ref)
    store_gradient = pltpu.make_async_copy(back_ref, gradient_ref, load_sem.at[3])
    store_gradient.start()
    finish(1)
    for row in range(3):
        rows = jnp.where(gain_owner, gains_back_ref[row : row + 1, :], 0.0)
        extra_send_ref[:, row, :] = split_dot(rows, gain_spread, 1)
    rows = jnp.where(bias_owner, bias_back_ref[...], 0.0)
    extra_send_ref[:, 3, :] = split_dot(rows, bias_spread, 1)
    extra_of = lambda flat: extra_send_ref.at[flat]
    t.small_send(1, extra_of, extras_ref)
    finish(2)
    finish(3)
    t.small_wait(1, extra_of, extras_ref)
    extra = jnp.sum(extras_ref[...], axis=0)
    extra_ref[...] = extra
    t.scatter_done(5)
    norm_ref[...] = squares_ref[...] + jnp.full(squares_ref.shape, jnp.sum(extra * extra), F32)
    norm_of = lambda flat: norm_ref
    t.small_send(2, norm_of, smalls_ref)
    store_block.wait()
    store_gradient.wait()
    t.small_wait(2, norm_of, smalls_ref)
    total_ref[...] = jnp.sum(smalls_ref[...], axis=0)


def exchanged_block(lengths, tokens, cotangent, norm_gains, expand_bias, pair_own, chunk_own):
    slots = tokens.shape[0]
    wides = lax.axis_size("wide")
    devices = wides * lax.axis_size("heads")
    deep = wides // 4
    rows = pair_own.shape[1]
    small = jnp.concatenate(
        [
            jnp.pad(norm_gains, ((0, 0), (0, 128 - norm_gains.shape[1]))),
            jnp.pad(expand_bias.astype(BF).astype(F32)[None], ((0, 4), (0, 128 - expand_bias.shape[0]))),
        ],
        axis=0,
    )
    vmem = pl.BlockSpec(memory_space=pltpu.VMEM)
    hbm = pl.BlockSpec(memory_space=pl.ANY)
    landings = lambda units, pairs, width: [
        pltpu.VMEM((2, 2, deep, 2, rows, width), BF),
        pltpu.VMEM((units, deep, rows, width), BF),
        pltpu.VMEM((pairs, 2, deep, rows, width), BF),
        pltpu.VMEM((units, deep - 1, rows, width), BF),
    ]
    tile = pltpu.VMEM((8, 128), F32)
    tiles = pltpu.VMEM((devices, 8, 128), F32)
    dma = pltpu.SemaphoreType.DMA
    gather_slots, scatter_slots = deep + 7, deep + 4
    block_output, token_gradient, pair_sum, chunk_sum, extra, total = pl.pallas_call(
        step_kernel,
        in_specs=[pl.BlockSpec(memory_space=pltpu.SMEM), hbm, hbm, vmem, hbm, hbm],
        out_specs=[hbm, hbm, vmem, vmem, vmem, vmem],
        out_shape=[
            jax.ShapeDtypeStruct((slots, D), F32),
            jax.ShapeDtypeStruct((slots, D), F32),
            jax.ShapeDtypeStruct((PAIRS, rows, 4 * PAIR), F32),
            jax.ShapeDtypeStruct((CHUNKS, rows, 2 * CHUNK), F32),
            jax.ShapeDtypeStruct((8, 128), F32),
            jax.ShapeDtypeStruct((8, 128), F32),
        ],
        scratch_shapes=[
            pltpu.VMEM((PAIRS, 2, deep, 2, 2, rows, 4 * PAIR), BF),
            pltpu.VMEM((CHUNKS, 2, deep, 2, 2, rows, 2 * CHUNK), BF),
        ]
        + landings(PAIRS, 2, 4 * PAIR)
        + landings(CHUNKS, CHUNKS, 2 * CHUNK)
        + [
            pltpu.VMEM((slots, D), BF), pltpu.VMEM((slots, D), BF),
            pltpu.VMEM((slots, D), F32), pltpu.VMEM((slots, D), F32),
            pltpu.VMEM((3, D), F32), pltpu.VMEM((1, FF), F32),
            pltpu.VMEM((3, D), F32), pltpu.VMEM((1, FF), F32),
            tiles, tiles, tiles, tile, tile,
            dma((UNITS, gather_slots)), dma((UNITS, gather_slots)),
            dma((UNITS, scatter_slots)), dma((UNITS, scatter_slots)),
            dma((UNITS,)), dma((3,)), dma((3,)), dma((3,)), dma((4,)),
        ]
        + attention_scratch(slots),
        compiler_params=pltpu.CompilerParams(
            vmem_limit_bytes=67043328, collective_id=0, has_side_effects=True
        ),
        name="step_block",
    )(lengths, tokens, cotangent, small, pair_own, chunk_own)
    grads = unpack_shards(pair_sum, chunk_sum) + (
        extra[3, : expand_bias.shape[0]],
        extra[:3, : norm_gains.shape[1]],
    )
    return block_output, token_gradient, grads, total[0, 0]


def optimizer_update(
    weight, raw_grad, factor, first, second, average, rate, decay, first_fix, second_fix, keep
):
    clipped = raw_grad * factor
    first_new = BETA_FIRST * first + (1.0 - BETA_FIRST) * clipped
    second_new = BETA_SECOND * second + (1.0 - BETA_SECOND) * clipped * clipped
    direction = first_new / first_fix / (jnp.sqrt(second_new / second_fix) + ADAM_EPS)
    weight_new = weight - rate * (direction + decay * weight)
    average_new = keep * average + (1.0 - keep) * weight_new
    return (clipped, first_new, second_new, weight_new, average_new)


def pack_shards(attend_weights, output_weights, expand_weights, reduce_weights):
    rows = attend_weights.shape[1]
    attend = attend_weights.astype(BF).reshape(3, rows, PAIRS, PAIR)
    attend = jnp.transpose(attend, (2, 1, 0, 3)).reshape(PAIRS, rows, 3 * PAIR)
    output = jnp.transpose(
        output_weights.astype(BF).T.reshape(rows, PAIRS, PAIR), (1, 0, 2)
    )
    expand = jnp.transpose(expand_weights.astype(BF).reshape(rows, CHUNKS, CHUNK), (1, 0, 2))
    reduce = jnp.transpose(reduce_weights.astype(BF).T.reshape(rows, CHUNKS, CHUNK), (1, 0, 2))
    return jnp.concatenate([attend, output], axis=2), jnp.concatenate([expand, reduce], axis=2)


def unpack_shards(pair_grads, chunk_grads):
    rows = pair_grads.shape[1]
    attend = jnp.transpose(
        pair_grads[:, :, : 3 * PAIR].reshape(PAIRS, rows, 3, PAIR), (2, 1, 0, 3)
    ).reshape(3, rows, HALF_E)
    join = lambda part: jnp.transpose(part, (1, 0, 2)).reshape(rows, -1)
    return (
        attend,
        join(pair_grads[:, :, 3 * PAIR :]).T,
        join(chunk_grads[:, :, :CHUNK]),
        join(chunk_grads[:, :, CHUNK:]).T,
    )


def gathered_block(lengths, tokens, cotangent, norm_gains, expand_bias, pair_own, chunk_own):
    both = ("heads", "wide")
    gains = lax.all_gather(norm_gains, both, axis=1, tiled=True)
    bias = lax.all_gather(expand_bias.astype(BF), both, axis=0, tiled=True).astype(F32)
    whole = lambda own: lax.all_gather(
        lax.all_gather(own, "wide", axis=1, tiled=True), "heads", axis=1
    )
    block_output, token_gradient, pair_grads, chunk_grads, bias_back, gains_back = local_block(
        lengths, tokens, cotangent, gains, bias[None, :], whole(pair_own), whole(chunk_own)
    )
    scatter = lambda part: lax.psum_scatter(
        lax.psum_scatter(part, "heads", scatter_dimension=1),
        "wide", scatter_dimension=1, tiled=True,
    ).astype(F32)
    grads = unpack_shards(scatter(pair_grads), scatter(chunk_grads)) + (
        lax.psum_scatter(bias_back[0], both, scatter_dimension=0, tiled=True),
        lax.psum_scatter(gains_back, both, scatter_dimension=1, tiled=True),
    )
    squares = jnp.sum(jnp.stack([jnp.sum(entry * entry) for entry in grads]))
    return block_output, token_gradient, grads, lax.psum(squares, both)


def body(
    tokens, cotangent, lengths, step_count,
    attend_weights, output_weights, expand_weights, reduce_weights, expand_bias, norm_gains,
    *moments,
):
    masters = (
        attend_weights, output_weights, expand_weights, reduce_weights, expand_bias, norm_gains,
    )
    firsts, seconds, averages = moments[:6], moments[6:12], moments[12:]
    pair_own, chunk_own = pack_shards(*masters[:4])
    wides = lax.axis_size("wide")
    aligned = wides % 8 == 0 and pair_own.shape[1] % 16 == 0 and lax.axis_size("heads") == 2
    block_output, token_gradient, grads, total_squares = (exchanged_block if aligned else gathered_block)(
        lengths, tokens[0], cotangent[0], norm_gains, expand_bias, pair_own, chunk_own
    )
    grad_norm = jnp.sqrt(total_squares)
    tokens_all = tokens.shape[1] * lax.axis_size("heads") * lax.axis_size("wide")
    limit = 0.02 * math.sqrt(tokens_all * D * FF)
    factor = jnp.minimum(1.0, limit / grad_norm)
    step_float = step_count[0].astype(F32)
    first_fix = 1.0 - jnp.power(BETA_FIRST, step_float)
    second_fix = 1.0 - jnp.power(BETA_SECOND, step_float)
    keep = jnp.minimum(AVERAGE_CAP, (1.0 + step_float) / (10.0 + step_float))
    results = [block_output[None], token_gradient[None], grad_norm.reshape(1)]
    for index in range(6):
        results.extend(
            optimizer_update(
                masters[index], grads[index], factor, firsts[index], seconds[index],
                averages[index], RATES[index], DECAYS[index], first_fix, second_fix, keep,
            )
        )
    return tuple(results)


def solution(mesh):
    both = ("heads", "wide")
    weight_specs = (
        P(None, "wide", "heads"), P("heads", "wide"), P("wide", "heads"), P("heads", "wide"),
        P(both), P(None, both),
    )
    image = P(both, None, None)
    return jax.shard_map(
        body,
        mesh=mesh,
        in_specs=(image, image, P(both), P()) + weight_specs * 4,
        out_specs=(image, image, P()) + tuple(spec for spec in weight_specs for _ in range(5)),
        check_vma=False,
    )
```

profile of v0, /device:TPU:0, one launch (start us, length us, event | category | flops | bytes accessed | tf_op | source)
XLA Modules:
  0.0 195.3 jit_solution(17534614954740186248)
XLA Ops:
  2.1 0.7 convert_bitcast_fusion.1
  2.8 1.3 select_maximum_fusion.small_ref
  4.1 0.9 bitcast_bitcast_fusion.3
  4.9 0.9 convert_element_type.25
  5.9 0.1 copy.63
  6.1 0.1 reshape.124
  6.2 0.7 pad_maximum_fusion.1.pair_own_ref
  6.8 1.0 convert_element_type.27
  7.8 1.0 convert_element_type.28
  8.8 0.7 pad_maximum_fusion.chunk_own_ref
  9.6 165.9 %step_block.1 = (f32[1024,768]{1,0:T(8,128)}, f32[1024,768]{1,0:T(8,128)}, f32[3,48,512]{2,1,0:T(8,128)}, f32[3,48,1024]{2,1,0:T(8,128)}, f32[8,128]{1,0:T(8,128)}, /*index=5*/f32[8,128]{1,0:T(8,128)}) custom-call(s32[1]{0:T(128)S(6)} %copy.84.length_ref, bf16[1024,768]{1,0:T(8,128)(2,1)} %bitcast.57, bf16[1024,768]{1,0:T(8,128)(2,1)} %bitcast.58, ...), custom_call_target="tpu_custom_call" | custom-call | tf_op jit(solution)/shard_map/step_block/pallas_call | solution.py:819
  175.5 0.0 copy-start.6
  175.5 1.2 slice.21
  177.4 1.3 multiply_add_fusion.10
  178.7 1.1 multiply_bitcast_fusion
  179.8 0.0 copy-start.2
  179.8 0.0 copy-start.8
  179.8 0.0 copy-start.9
  179.9 0.0 copy-start.10
  179.9 0.0 copy-start.4
  179.9 1.5 multiply_add_fusion.8
  181.4 1.0 slice_multiply_fusion
  182.4 1.8 multiply_add_fusion.6
  184.2 0.1 mul.354
  184.3 0.0 copy-start.3
  184.3 0.0 copy-start.11
  184.3 0.0 copy-start.12
  184.3 0.2 copy.67
  184.5 0.1 mul.356
  184.6 0.0 copy-start.7
  184.6 0.0 copy-start.13
  184.6 0.0 copy-start.5
  184.7 0.0 copy-done.6
  184.7 2.4 %multiply_add_fusion.4 = (f32[3,48,384]{2,1,0:T(8,128)}, f32[3,48,384]{2,1,0:T(8,128)}, f32[3,48,384]{2,1,0:T(8,128)}, f32[3,48,384]{2,1,0:T(8,128)}) fusion(f32[3,48,384]{2,1,0:T(8,128)} %param.50, f32[]{:T(128)S(6)} %sub.43, f32[]{:T(128)} %bitcast.16, f32[3,48,384]{2,1,0:T(8,128)S(1)} %copy-done.6, f32[]{:T(128)} %bitcast.15, f32[]{:T(128)} %bitcast.14, ...), kind=kLoop, calls=%fused_computation.15 | loop fusion | flops 995328 | bytes 1990672 | tf_op jit(solution)/shard_map/add | solution.py:868
  187.0 0.0 copy-done.2
  187.1 0.0 copy-done.8
  187.1 0.0 copy-done.9
  187.1 0.0 copy-done.10
  187.1 1.2 multiply_add_fusion.2
  188.2 0.0 copy-done.4
  188.2 0.0 copy-done.3
  188.3 0.0 copy-done.11
  188.3 0.0 copy-done.12
  188.3 1.2 multiply_add_fusion
  189.4 0.0 copy-done.1
  189.5 1.7 copy.86
  191.1 1.4 copy-done
  192.5 1.7 copy.87
  (10 shorter events, 0.1 us)
Async XLA Ops:
  175.5 9.2 %copy-start.6 = (f32[3,48,384]{2,1,0:T(8,128)S(1)}, f32[3,48,384]{2,1,0:T(8,128)}, u32[]{:S(2)}) copy-start(f32[3,48,384]{2,1,0:T(8,128)} %param.32) | copy-start | bytes 663556
  179.8 7.2 %copy-start.2 = (f32[48,1536]{1,0:T(8,128)S(1)}, f32[48,1536]{1,0:T(8,128)}, u32[]{:S(2)}) copy-start(f32[48,1536]{1,0:T(8,128)} %param.34) | copy-start | bytes 884740
  179.8 7.2 %copy-start.8 = (f32[48,1536]{1,0:T(8,128)S(1)}, f32[48,1536]{1,0:T(8,128)}, u32[]{:S(2)}) copy-start(f32[48,1536]{1,0:T(8,128)} %param.52) | copy-start | bytes 884740
  179.8 7.2 %copy-start.9 = (f32[48,1536]{1,0:T(8,128)S(1)}, f32[48,1536]{1,0:T(8,128)}, u32[]{:S(2)}) copy-start(f32[48,1536]{1,0:T(8,128)} %param.46) | copy-start | bytes 884740
  179.9 7.2 %copy-start.10 = (f32[48,1536]{1,0:T(8,128)S(1)}, f32[48,1536]{1,0:T(8,128)}, u32[]{:S(2)}) copy-start(f32[48,1536]{1,0:T(8,128)} %param.40) | copy-start | bytes 884740
  179.9 8.3 %copy-start.4 = (f32[3,6,8,512]{3,2,0,1:T(8,128)}, f32[3,6,8,512]{3,2,0,1:T(8,128)S(1)}, u32[]{:S(2)}) copy-start(f32[3,6,8,512]{3,2,0,1:T(8,128)S(1)} %copy.76) | copy-start | bytes 884740
  184.3 4.0 %copy-start.3 = (f32[1536,48]{0,1:T(8,128)S(1)}, f32[1536,48]{0,1:T(8,128)}, u32[]{:S(2)}) copy-start(f32[1536,48]{0,1:T(8,128)} %param.35) | copy-start | bytes 884740
  184.3 4.0 %copy-start.11 = (f32[1536,48]{0,1:T(8,128)S(1)}, f32[1536,48]{0,1:T(8,128)}, u32[]{:S(2)}) copy-start(f32[1536,48]{0,1:T(8,128)} %param.53) | copy-start | bytes 884740
  184.3 4.0 %copy-start.12 = (f32[1536,48]{0,1:T(8,128)S(1)}, f32[1536,48]{0,1:T(8,128)}, u32[]{:S(2)}) copy-start(f32[1536,48]{0,1:T(8,128)} %param.47) | copy-start | bytes 884740
  184.6 4.9 %copy-start.7 = (f32[3,48,384]{2,1,0:T(8,128)}, f32[3,48,384]{2,1,0:T(8,128)S(1)}, u32[]{:S(2)}) copy-start(f32[3,48,384]{2,1,0:T(8,128)S(1)} %mul.356) | copy-start | bytes 663556
  184.6 3.7 %copy-start.13 = (f32[1536,48]{0,1:T(8,128)S(1)}, f32[1536,48]{0,1:T(8,128)}, u32[]{:S(2)}) copy-start(f32[1536,48]{0,1:T(8,128)} %param.41) | copy-start | bytes 884740
  184.6 4.8 %copy-start.5 = (f32[3,6,8,512]{3,2,0,1:T(8,128)}, f32[3,6,8,512]{3,2,0,1:T(8,128)S(1)}, u32[]{:S(2)}) copy-start(f32[3,6,8,512]{3,2,0,1:T(8,128)S(1)} %copy.75) | copy-start | bytes 884740
  187.0 2.4 %copy-start.1 = (f32[1024,768]{1,0:T(8,128)S(1)}, f32[1024,768]{1,0:T(8,128)}, u32[]{:S(2)}) copy-start(f32[1024,768]{1,0:T(8,128)} %get-tuple-element.39) | copy-start | bytes 9437188
  189.5 3.0 %copy-start = (f32[1024,768]{1,0:T(8,128)S(1)}, f32[1024,768]{1,0:T(8,128)}, u32[]{:S(2)}) copy-start(f32[1024,768]{1,0:T(8,128)} %get-tuple-element.40) | copy-start | bytes 9437188
where the time goes:
time: 196 us; the launch traced here: 195 us
  Pallas kernels  166 us (85%)
  other arithmetic  18.5 us (9%)
  local copies, waits for them, and re-layouts  6.69 us (3%)
  between operations  4.2 us (2%)
    pallas_call x1, Pallas kernels, exchanged_block(): pl.pallas_call(step_kernel, in_specs=[pl.BlockSpec(memory_space=pltpu.SME...  166 us
    add x6, other arithmetic, optimizer_update(): average_new = keep * average + (1.0 - keep) * weight_new  9.31 us
    unnamed x30, local copies, waits for them, and re-layouts  4.79 us

commit v1 on v0

--- a/solution.py
+++ b/solution.py
@@ -45,18 +45,20 @@
     return center * inverse, inverse
 
 
-def head_mean(values):
+def head_mean(values, exact=False):
     width = values.shape[1]
     row = lax.broadcasted_iota(jnp.int32, (width, width), 0) // HEAD_DIM
     column = lax.broadcasted_iota(jnp.int32, (width, width), 1) // HEAD_DIM
     block = jnp.where(row == column, 1.0 / HEAD_DIM, 0.0).astype(BF)
     high = values.astype(BF)
-    rest = (values - high.astype(F32)).astype(BF)
-    return dot(high, block, 1, 0) + dot(rest, block, 1, 0)
+    mean = dot(high, block, 1, 0)
+    if not exact:
+        return mean
+    return mean + dot((values - high.astype(F32)).astype(BF), block, 1, 0)
 
 
 def head_norm(values):
-    center = values - head_mean(values)
+    center = values - head_mean(values, True)
     inverse = lax.rsqrt(head_mean(center * center) + NORM_EPS)
     return center * inverse, inverse
 
@@ -377,11 +379,6 @@
             return self.pair.at[PAIR_UNITS.index(unit)]
         return self.chunk.at[CHUNK_UNITS.index(unit)]
 
-    def own(self, unit):
-        if unit in PAIR_UNITS:
-            return self.pair_own.at[PAIR_UNITS.index(unit)]
-        return self.chunk_own.at[CHUNK_UNITS.index(unit)]
-
     def landing(self, unit, stage):
         pair = unit in PAIR_UNITS
         landing = (self.pair_landing if pair else self.chunk_landing)[stage]
@@ -412,10 +409,10 @@
         )
 
     def gather_copy(self, unit, slot):
-        buf, own, half = self.buffer(unit), self.own(unit), self.deep // 2
+        buf, half = self.buffer(unit), self.deep // 2
         h, a, b, c = self.h, self.a, self.b, self.c
         if slot < self.deep - 1:
-            return self.copy(own, buf.at[h, a, b, c], self.gather_sems, unit, slot, self.along(slot + 1))
+            return self.copy(buf.at[h, a, b, c], buf.at[h, a, b, c], self.gather_sems, unit, slot, self.along(slot + 1))
         slot -= self.deep - 1
         region, device = (
             (lambda r: r.at[h, :, b, c], self.beside("h")),
@@ -439,18 +436,40 @@
         for slot in slots:
             self.gather_copy(unit, slot).wait_recv()
 
-    def local_copy(self, unit):
-        return pltpu.make_async_copy(
-            self.own(unit), self.buffer(unit).at[self.h, self.a, self.b, self.c], self.local_sem.at[unit]
-        )
+    def pieces(self, unit):
+        cut = lambda place: pl.ds(place * PAIR, PAIR)
+        attend, output, expand, reduce = self.shards
+        if unit in PAIR_UNITS:
+            place = PAIR_UNITS.index(unit)
+            return [attend.at[part, :, cut(place)] for part in range(3)] + [output.at[:, cut(place)]]
+        first = CHUNK_UNITS.index(unit) * (CHUNK // PAIR)
+        return [ref.at[:, cut(first + place)] for ref in (expand, reduce) for place in range(CHUNK // PAIR)]
+
+    def staged(self, unit):
+        rows, count = self.pair.shape[5], len(self.pieces(unit))
+        half, first = ((0, 0), (0, 4), (0, 8), (1, 0), (1, 8), (0, 16))[unit]
+        return self.stage.at[half, pl.ds(first * rows, count * rows), :]
+
+    def load(self, unit):
+        rows = self.pair.shape[5]
+        for place, piece in enumerate(self.pieces(unit)):
+            pltpu.make_async_copy(
+                piece, self.staged(unit).at[pl.ds(place * rows, rows), :], self.local_sem.at[unit]
+            ).start()
+
+    def pack(self, unit):
+        rows, staged, buf = self.pair.shape[5], self.staged(unit), self.buffer(unit)
+        pltpu.make_async_copy(staged, staged, self.local_sem.at[unit]).wait()
+        for place in range(len(self.pieces(unit))):
+            buf[self.h, self.a, self.b, self.c, :, place * PAIR : (place + 1) * PAIR] = staged[
+                place * rows : (place + 1) * rows, :
+            ].astype(BF)
 
     def gather_deep(self, unit):
         self.gather_start(unit, range(self.deep - 1))
-        self.local_copy(unit).start()
 
     def gather_sides(self, unit):
         n = self.deep - 1
-        self.local_copy(unit).wait()
         self.gather_wait(unit, range(n))
         self.gather_start(unit, (n, n + 1, n + 4))
 
@@ -602,7 +621,8 @@
 
 
 def step_kernel(
-    length_ref, tokens_ref, cotangent_ref, small_ref, pair_own_ref, chunk_own_ref,
+    length_ref, tokens_ref, cotangent_ref, own_gains_ref, own_bias_ref,
+    attend_ref, output_ref, expand_ref, reduce_ref,
     block_ref, gradient_ref, pair_sum_ref, chunk_sum_ref, extra_ref, total_ref,
     pair_ref, chunk_ref, pair_land0, pair_land1, pair_land2, pair_land3,
     chunk_land0, chunk_land1, chunk_land2, chunk_land3,
@@ -613,7 +633,7 @@
 ):
     t = Traffic(
         dict(
-            pair=pair_ref, chunk=chunk_ref, pair_own=pair_own_ref, chunk_own=chunk_own_ref,
+            pair=pair_ref, chunk=chunk_ref, shards=(attend_ref, output_ref, expand_ref, reduce_ref), stage=work[4],
             pair_landing=(pair_land0, pair_land1, pair_land2, pair_land3),
             chunk_landing=(chunk_land0, chunk_land1, chunk_land2, chunk_land3),
             pair_sum=pair_sum_ref, chunk_sum=chunk_sum_ref, squares=squares_ref,
@@ -628,14 +648,20 @@
     load_cotangent = lambda: pltpu.make_async_copy(cotangent_ref, upstream_ref, load_sem.at[1])
     load_tokens().start()
     load_cotangent().start()
+    for unit in range(UNITS):
+        t.load(unit)
     barrier = pltpu.get_barrier_semaphore()
     t.everyone(
         lambda flat, device: pl.semaphore_signal(barrier, inc=1, device_id=device, device_id_type=MESH)
     )
+    t.pack(0)
+    norm_ref[...] = jnp.zeros_like(norm_ref)
+    norm_ref[0:3, 0:gain_width] = own_gains_ref[...]
+    norm_ref[3:4, 0:bias_width] = own_bias_ref[...].astype(BF).astype(F32)
     pl.semaphore_wait(barrier, devices - 1)
 
     t.gather_deep(0)
-    small_of = lambda flat: small_ref
+    small_of = lambda flat: norm_ref
     t.small_send(0, small_of, smalls_ref)
     squares_ref[...] = jnp.zeros_like(squares_ref)
     extra_send_ref[...] = jnp.zeros_like(extra_send_ref)
@@ -650,6 +676,8 @@
         out_ref[rows, :] = inputs
         back_ref[rows, :], _ = row_norm(inputs)
 
+    for unit in range(1, UNITS):
+        t.pack(unit)
     over_rows(slots, prepare)
     t.gather_sides(0)
     t.gather_deep(1)
@@ -791,19 +819,13 @@
     total_ref[...] = jnp.sum(smalls_ref[...], axis=0)
 
 
-def exchanged_block(lengths, tokens, cotangent, norm_gains, expand_bias, pair_own, chunk_own):
+def exchanged_block(lengths, tokens, cotangent, masters):
+    attend, output, expand, reduce, bias, gains = turned(masters)
     slots = tokens.shape[0]
     wides = lax.axis_size("wide")
     devices = wides * lax.axis_size("heads")
     deep = wides // 4
-    rows = pair_own.shape[1]
-    small = jnp.concatenate(
-        [
-            jnp.pad(norm_gains, ((0, 0), (0, 128 - norm_gains.shape[1]))),
-            jnp.pad(expand_bias.astype(BF).astype(F32)[None], ((0, 4), (0, 128 - expand_bias.shape[0]))),
-        ],
-        axis=0,
-    )
+    rows = attend.shape[1]
     vmem = pl.BlockSpec(memory_space=pltpu.VMEM)
     hbm = pl.BlockSpec(memory_space=pl.ANY)
     landings = lambda units, pairs, width: [
@@ -818,7 +840,7 @@
     gather_slots, scatter_slots = deep + 7, deep + 4
     block_output, token_gradient, pair_sum, chunk_sum, extra, total = pl.pallas_call(
         step_kernel,
-        in_specs=[pl.BlockSpec(memory_space=pltpu.SMEM), hbm, hbm, vmem, hbm, hbm],
+        in_specs=[pl.BlockSpec(memory_space=pltpu.SMEM), hbm, hbm, vmem, vmem, hbm, hbm, hbm, hbm],
         out_specs=[hbm, hbm, vmem, vmem, vmem, vmem],
         out_shape=[
             jax.ShapeDtypeStruct((slots, D), F32),
@@ -849,12 +871,8 @@
             vmem_limit_bytes=67043328, collective_id=0, has_side_effects=True
         ),
         name="step_block",
-    )(lengths, tokens, cotangent, small, pair_own, chunk_own)
-    grads = unpack_shards(pair_sum, chunk_sum) + (
-        extra[3, : expand_bias.shape[0]],
-        extra[:3, : norm_gains.shape[1]],
-    )
-    return block_output, token_gradient, grads, total[0, 0]
+    )(lengths, tokens, cotangent, gains, bias, attend, output, expand, reduce)
+    return block_output, token_gradient, (pair_sum, chunk_sum, extra, total)
 
 
 def optimizer_update(
@@ -867,6 +885,94 @@
     weight_new = weight - rate * (direction + decay * weight)
     average_new = keep * average + (1.0 - keep) * weight_new
     return (clipped, first_new, second_new, weight_new, average_new)
+
+
+def update_kernel(limit, step_ref, pair_ref, chunk_ref, extra_ref, total_ref, block_in, gradient_in, *refs):
+    masters, firsts, seconds, averages = (refs[6 * group : 6 * group + 6] for group in range(4))
+    block_out, gradient_out, norm_ref = refs[24:27]
+    results = [refs[27 + 5 * index : 32 + 5 * index] for index in range(6)]
+    block_out[...] = block_in[...]
+    gradient_out[...] = gradient_in[...]
+
+    step = pl.program_id(0)
+    norm = jnp.sqrt(total_ref[0:1, :])
+    factor = jnp.minimum(1.0, limit / norm)
+    step_float = jnp.full((1, PAIR), step_ref[0].astype(F32), F32)
+    first_fix = 1.0 - jnp.exp(step_float * math.log(BETA_FIRST))
+    second_fix = 1.0 - jnp.exp(step_float * math.log(BETA_SECOND))
+    keep = jnp.minimum(AVERAGE_CAP, (1.0 + step_float) / (10.0 + step_float))
+
+    def apply(index, where, raw_grad):
+        lanes = raw_grad.shape[1]
+        new = optimizer_update(
+            masters[index][where], raw_grad, factor[:, :lanes], firsts[index][where],
+            seconds[index][where], averages[index][where], RATES[index], DECAYS[index],
+            first_fix[:, :lanes], second_fix[:, :lanes], keep[:, :lanes],
+        )
+        for ref, value in zip(results[index], new):
+            ref[where] = value
+
+    everything = slice(None)
+    cut = lambda place: slice(place * PAIR, (place + 1) * PAIR)
+
+    @pl.when(step < PAIRS)
+    def _():
+        for part in range(3):
+            apply(0, (part,), pair_ref[0, :, cut(part)])
+        apply(1, (everything,), pair_ref[0, :, cut(3)])
+        for place in range(CHUNK // PAIR):
+            apply(2, (everything, cut(place)), chunk_ref[0, :, cut(place)])
+            apply(3, (everything, cut(place)), chunk_ref[0, :, cut(CHUNK // PAIR + place)])
+
+    @pl.when(step == PAIRS)
+    def _():
+        norm_ref[0] = norm[0, 0]
+        apply(4, (everything,), extra_ref[3:4, : masters[4].shape[1]])
+        apply(5, (everything,), extra_ref[0:3, : masters[5].shape[1]])
+
+
+def turned(arrays):
+    attend, output, expand, reduce, bias, gains = arrays
+    return [attend, output.T, expand, reduce.T, bias[None, :], gains]
+
+
+def turned_back(arrays):
+    attend, output, expand, reduce, bias, gains = arrays
+    return [attend, output.T, expand, reduce.T, bias[0], gains]
+
+
+def updated_weights(step_count, limit, sums, block_output, token_gradient, groups):
+    slots = block_output.shape[0]
+    arrays = [entry for group in groups for entry in turned(group)]
+    shapes = [jax.ShapeDtypeStruct(entry.shape, F32) for entry in arrays[:6] for _ in range(5)]
+    steps = PAIRS + 1
+    whole = lambda entry: pl.BlockSpec(entry.shape, lambda index: (0,) * len(entry.shape))
+    unit = lambda index: jnp.minimum(index, PAIRS - 1)
+
+    def part(entry):
+        if entry.shape[0] < 8 and len(entry.shape) == 2:
+            return whole(entry)
+        block = entry.shape[:-1] + (entry.shape[-1] // PAIRS,)
+        return pl.BlockSpec(block, lambda index: (0,) * (len(block) - 1) + (unit(index),))
+
+    unit_part = lambda entry: pl.BlockSpec((1,) + entry.shape[1:], lambda index: (unit(index), 0, 0))
+    rows = pl.BlockSpec((slots // steps, D), lambda index: (index, 0))
+    smem = pl.BlockSpec(memory_space=pltpu.SMEM)
+    image = jax.ShapeDtypeStruct((slots, D), F32)
+    out = pl.pallas_call(
+        partial(update_kernel, limit),
+        grid=(steps,),
+        in_specs=[smem]
+        + [unit_part(entry) for entry in sums[:2]]
+        + [whole(entry) for entry in sums[2:]]
+        + [rows, rows]
+        + [part(entry) for entry in arrays],
+        out_specs=[rows, rows, smem] + [part(entry) for entry in shapes],
+        out_shape=[image, image, jax.ShapeDtypeStruct((1,), F32)] + shapes,
+        name="update_weights",
+    )(step_count, *sums, block_output, token_gradient, *arrays)
+    fields = [turned_back(out[3 + field :: 5]) for field in range(5)]
+    return out[:3], [fields[field][index] for index in range(6) for field in range(5)]
 
 
 def pack_shards(attend_weights, output_weights, expand_weights, reduce_weights):
@@ -926,15 +1032,20 @@
         attend_weights, output_weights, expand_weights, reduce_weights, expand_bias, norm_gains,
     )
     firsts, seconds, averages = moments[:6], moments[6:12], moments[12:]
+    wides = lax.axis_size("wide")
+    tokens_all = tokens.shape[1] * lax.axis_size("heads") * wides
+    limit = 0.02 * math.sqrt(tokens_all * D * FF)
+    if wides % 8 == 0 and attend_weights.shape[1] % 16 == 0 and lax.axis_size("heads") == 2:
+        block_output, token_gradient, sums = exchanged_block(lengths, tokens[0], cotangent[0], masters)
+        (block_output, token_gradient, grad_norm), updated = updated_weights(
+            step_count, limit, sums, block_output, token_gradient, (masters, firsts, seconds, averages)
+        )
+        return (block_output[None], token_gradient[None], grad_norm, *updated)
     pair_own, chunk_own = pack_shards(*masters[:4])
-    wides = lax.axis_size("wide")
-    aligned = wides % 8 == 0 and pair_own.shape[1] % 16 == 0 and lax.axis_size("heads") == 2
-    block_output, token_gradient, grads, total_squares = (exchanged_block if aligned else gathered_block)(
+    block_output, token_gradient, grads, total_squares = gathered_block(
         lengths, tokens[0], cotangent[0], norm_gains, expand_bias, pair_own, chunk_own
     )
     grad_norm = jnp.sqrt(total_squares)
-    tokens_all = tokens.shape[1] * lax.axis_size("heads") * lax.axis_size("wide")
-    limit = 0.02 * math.sqrt(tokens_all * D * FF)
     factor = jnp.minimum(1.0, limit / grad_norm)
     step_float = step_count[0].astype(F32)
     first_fix = 1.0 - jnp.power(BETA_FIRST, step_float)

time: 196 us -> 175 us (0.89)
  other arithmetic: 18.5 us -> 0 us
  local copies, waits for them, and re-layouts: 6.69 us -> 0 us
  Pallas kernels: 166 us -> 172 us
  between operations: 4.2 us -> 2.14 us
    add x6 -> x0, other arithmetic: 9.31 us -> none  [optimizer_update(): average_new = keep * average + (1.0 - keep) * weight_new]
    pallas_call x0 -> x1, Pallas kernels: none -> 9.23 us  [updated_weights(): pl.pallas_call(partial(update_kernel, limit), grid=(steps,), in_specs=[sm...]
    unnamed x30 -> x0, local copies, waits for them, and re-layouts: 4.79 us -> none
    convert_element_type x3 -> x0, other arithmetic: 2.91 us -> none  [the longest x1 0.98 us: pack_shards(): reduce_weights.astype(BF).T.reshape(rows, CHUNKS, CHUNK)]
    pallas_call x1, Pallas kernels: 166 us -> 163 us  [exchanged_block(): pl.pallas_call(step_kernel, in_specs=[pl.BlockSpec(memory_space=pltpu.SME...]
    concatenate x3 -> x0, other arithmetic: 2.7 us -> none  [the longest x1 1.28 us: exchanged_block(): jnp.concatenate([jnp.pad(norm_gains, ((0, 0), (0, 128 - norm_gains.shape[...]
where the time goes in v1:
time: 175 us; the launch traced here: 174 us
  Pallas kernels  172 us (98%)
  between operations  2.14 us (1%)
    pallas_call x1, Pallas kernels, exchanged_block(): pl.pallas_call(step_kernel, in_specs=[pl.BlockSpec(memory_space=pltpu.SME...  163 us
    pallas_call x1, Pallas kernels, updated_weights(): pl.pallas_call(partial(update_kernel, limit), grid=(steps,), in_specs=[sm...  9.23 us

profile of v1, /device:TPU:0, one launch (start us, length us, event | category | flops | bytes accessed | tf_op | source)
XLA Modules:
  0.0 174.4 jit_solution(8148269627927008680)
XLA Ops:
  2.0 163.1 %step_block.1 = (f32[1024,768]{1,0:T(8,128)}, f32[1024,768]{1,0:T(8,128)}, f32[3,48,512]{2,1,0:T(8,128)}, f32[3,48,1024]{2,1,0:T(8,128)}, f32[8,128]{1,0:T(8,128)}, /*index=5*/f32[8,128]{1,0:T(8,128)}) custom-call(s32[1]{0:T(128)S(6)} %copy.61.length_ref, bf16[1024,768]{1,0:T(8,128)(2,1)} %bitcast.31, bf16[1024,768]{1,0:T(8,128)(2,1)} %bitcast.32, ...), custom_call_target="tpu_custom_call" | custom-call | tf_op jit(solution)/shard_map/step_block/pallas_call | solution.py:841
  165.0 9.2 %update_weights.1 = (f32[1024,768]{1,0:T(8,128)}, f32[1024,768]{1,0:T(8,128)}, f32[1]{0:T(128)}, f32[3,48,384]{2,1,0:T(8,128)}, f32[3,48,384]{2,1,0:T(8,128)}, /...) custom-call(s32[1]{0:T(128)S(6)} %copy.62.step_ref, ...), custom_call_target="tpu_custom_call" | custom-call | tf_op jit(solution)/shard_map/update_weights/pallas_call | solution.py:962

commit v2 on v1

--- a/solution.py
+++ b/solution.py
@@ -518,6 +518,9 @@
 
     def add(self, unit, where, *parts):
         buf = self.buffer(unit)
+        if len(parts) == 1:
+            buf[where] = buf[where] + parts[0]
+            return
         total = buf[where].astype(F32)
         for part in parts:
             total = total + part.astype(F32)

time: 175 us -> 174 us (level)
  no operation moved by 1% of the time
where the time goes in v2:
time: 174 us; the launch traced here: 173 us
  Pallas kernels  171 us (98%)
  between operations  2.14 us (1%)
    pallas_call x1, Pallas kernels, exchanged_block(): pl.pallas_call(step_kernel, in_specs=[pl.BlockSpec(memory_space=pltpu.SME...  162 us
    pallas_call x1, Pallas kernels, updated_weights(): pl.pallas_call(partial(update_kernel, limit), grid=(steps,), in_specs=[sm...  9.23 us

profile of v2, /device:TPU:0, one launch (start us, length us, event | category | flops | bytes accessed | tf_op | source)
XLA Modules:
  0.0 173.5 jit_solution(17230096905745767548)
XLA Ops:
  2.0 162.1 %step_block.1 = (f32[1024,768]{1,0:T(8,128)}, f32[1024,768]{1,0:T(8,128)}, f32[3,48,512]{2,1,0:T(8,128)}, f32[3,48,1024]{2,1,0:T(8,128)}, f32[8,128]{1,0:T(8,128)}, /*index=5*/f32[8,128]{1,0:T(8,128)}) custom-call(s32[1]{0:T(128)S(6)} %copy.61.length_ref, bf16[1024,768]{1,0:T(8,128)(2,1)} %bitcast.31, bf16[1024,768]{1,0:T(8,128)(2,1)} %bitcast.32, ...), custom_call_target="tpu_custom_call" | custom-call | tf_op jit(solution)/shard_map/step_block/pallas_call | solution.py:844
  164.1 9.2 %update_weights.1 = (f32[1024,768]{1,0:T(8,128)}, f32[1024,768]{1,0:T(8,128)}, f32[1]{0:T(128)}, f32[3,48,384]{2,1,0:T(8,128)}, f32[3,48,384]{2,1,0:T(8,128)}, /...) custom-call(s32[1]{0:T(128)S(6)} %copy.62.step_ref, ...), custom_call_target="tpu_custom_call" | custom-call | tf_op jit(solution)/shard_map/update_weights/pallas_call | solution.py:965
